TPU v7x, 256 devices: a whole 4x4x8 slice. The times are simulated.
256 devices in a mesh: dp: 16 (over z, core), expert: 16 (over x, y).
Axes of the slice: x: 4, y: 4, z: 8, core: 2. Of those that a mesh axis runs over, the one named last changes fastest.
Arguments:
- saved_input: bfloat16 [32768, 2048], P(('dp', 'expert')), parts along dimension 0, may hold values from -6 to 6
- grad_out: bfloat16 [32768, 2048], P(('dp', 'expert')), parts along dimension 0, may hold values from -6 to 6
- routes: int32 [32768, 8], P(('dp', 'expert')), parts along dimension 0, may hold values from 0 to 15, all different within a row
- route_gates: bfloat16 [32768, 8], P(('dp', 'expert')), parts along dimension 0, may hold values from 0.049804688 to 0.5
- gate_proj: bfloat16 [16, 2048, 768], P('expert'), may hold values from -0.125 to 0.125
- up_proj: bfloat16 [16, 2048, 768], P('expert'), may hold values from -0.125 to 0.125
- down_proj: bfloat16 [16, 768, 2048], P('expert'), may hold values from -0.21875 to 0.21875
Outputs:
- grad_in: bfloat16 [32768, 2048], P(('dp', 'expert')), parts along dimension 0
There are 16 independent parts, one for each index of `dp`. A program takes and returns all parts, laid end to end along the dimension named above; an argument that names none is the same for every part. Nothing has to cross between parts.
Inputs may be any that keep to these rules, and one draw needn't show every extreme that they name: `routes`: each token names 8 different experts, and every expert is named by some token.
All inputs are finite; a program needn't handle non-finite values.
Results may differ from a plain program's by a relative error of at most 0.0057.
Values may be sent and summed in bfloat16 or wider, within the bound.
A program may use at most 128 MiB of HBM per device.

v0:
```python
import functools

import jax
import jax.numpy as jnp
from jax import lax
from jax.experimental import pallas as pl
from jax.experimental.pallas import tpu as pltpu
from jax.sharding import PartitionSpec as P

CAP = 56
LANES = 128
MESH_ID = pl.DeviceIdType.MESH


def pair_ranks(ordered, experts):
    labels = jnp.arange(experts, dtype=jnp.int32)
    matches = (ordered[..., None] == labels).astype(jnp.int32)
    earlier = jnp.cumsum(matches, axis=-2) - matches
    return jnp.sum(earlier * matches, axis=-1)


def expert_block(x, g, w, wg_ref, wu_ref, wd_ref):
    nt = (((1,), (1,)), ((), ()))
    gate_pre = jnp.dot(x, wg_ref[...], preferred_element_type=jnp.float32)
    up_pre = jnp.dot(x, wu_ref[...], preferred_element_type=jnp.float32)
    back_grad = lax.dot_general(g, wd_ref[...], nt, preferred_element_type=jnp.float32)
    scaled = w[:, 0:1].astype(jnp.float32) * back_grad
    sigmoid_gate = 1.0 / (1.0 + jnp.exp(-gate_pre))
    gate_grad = (scaled * up_pre * sigmoid_gate * (1.0 + gate_pre * (1.0 - sigmoid_gate))).astype(
        jnp.bfloat16
    )
    up_grad = (scaled * gate_pre * sigmoid_gate).astype(jnp.bfloat16)
    summed = lax.dot_general(gate_grad, wg_ref[...], nt, preferred_element_type=jnp.float32)
    summed = summed + lax.dot_general(up_grad, wu_ref[...], nt, preferred_element_type=jnp.float32)
    return summed.astype(jnp.bfloat16)


def moe_kernel(n, sx, sg, sw, wg, wu, wd, ret, rx, rg, rw, ob, dsend, drecv, bsend, brecv, lsem):
    me = lax.axis_index("expert")

    def peer(d):
        return {"expert": lax.rem(me + d, n)}

    def back_peer(d):
        return {"expert": lax.rem(me + n - d, n)}

    barrier = pltpu.get_barrier_semaphore()
    for d in range(1, n):
        pl.semaphore_signal(barrier, 1, device_id=peer(d), device_id_type=MESH_ID)
    pl.semaphore_wait(barrier, n - 1)

    srcs = (sx, sg, sw)
    dsts = (rx, rg, rw)

    def dispatch(k, d):
        return pltpu.make_async_remote_copy(
            srcs[k].at[d], dsts[k].at[d], dsend.at[k, d], drecv.at[k, d],
            device_id=peer(d), device_id_type=MESH_ID,
        )

    def give_back(d):
        return pltpu.make_async_remote_copy(
            ob.at[d], ret.at[d], bsend.at[d], brecv.at[d],
            device_id=back_peer(d), device_id_type=MESH_ID,
        )

    local_in = [pltpu.make_async_copy(srcs[k].at[0], dsts[k].at[0], lsem.at[k]) for k in range(3)]
    for c in local_in:
        c.start()
    for d in range(1, n):
        for k in range(3):
            dispatch(k, d).start()

    for c in local_in:
        c.wait()
    ob[0] = expert_block(rx[0], rg[0], rw[0], wg, wu, wd)
    local_out = pltpu.make_async_copy(ob.at[0], ret.at[0], lsem.at[3])
    local_out.start()

    def step(d, carry):
        for k in range(3):
            dispatch(k, d).wait_recv()
        ob[d] = expert_block(rx[d], rg[d], rw[d], wg, wu, wd)
        give_back(d).start()
        return carry

    lax.fori_loop(1, n, step, 0)

    def drain(d, carry):
        for k in range(3):
            dispatch(k, d).wait_send()
        give_back(d).wait_send()
        give_back(d).wait_recv()
        return carry

    lax.fori_loop(1, n, drain, 0)
    local_out.wait()


def exchange(send_x, send_g, send_w, wg, wu, wd):
    n, cap, features = send_x.shape
    ff = wg.shape[1]
    vmem = pltpu.MemorySpace.VMEM
    flops = 2 * n * cap * features * ff * 5
    return pl.pallas_call(
        functools.partial(moe_kernel, n),
        out_shape=jax.ShapeDtypeStruct((n, cap, features), jnp.bfloat16),
        in_specs=[pl.BlockSpec(memory_space=pl.ANY)] * 3 + [pl.BlockSpec(memory_space=vmem)] * 3,
        out_specs=pl.BlockSpec(memory_space=pl.ANY),
        scratch_shapes=[
            pltpu.VMEM((n, cap, features), jnp.bfloat16),
            pltpu.VMEM((n, cap, features), jnp.bfloat16),
            pltpu.VMEM((n, cap, LANES), jnp.bfloat16),
            pltpu.VMEM((n, cap, features), jnp.bfloat16),
            pltpu.SemaphoreType.DMA((3, n)),
            pltpu.SemaphoreType.DMA((3, n)),
            pltpu.SemaphoreType.DMA((n,)),
            pltpu.SemaphoreType.DMA((n,)),
            pltpu.SemaphoreType.DMA((4,)),
        ],
        compiler_params=pltpu.CompilerParams(
            collective_id=0, has_side_effects=True, vmem_limit_bytes=60 * 1024 * 1024
        ),
        cost_estimate=pl.CostEstimate(
            flops=flops, transcendentals=n * cap * ff, bytes_accessed=n * cap * features * 2 * 4
        ),
    )(send_x, send_g, send_w, wg, wu, wd)


def body(saved_input, grad_out, routes, route_gates, gate_proj, up_proj, down_proj):
    devices = lax.axis_size("expert")
    local_experts = gate_proj.shape[0]
    assert local_experts == 1
    experts = devices * local_experts
    tok_rows, features = saved_input.shape
    top_count = routes.shape[1]
    slot_count = devices * CAP
    me = lax.axis_index("expert")
    ordered = jnp.swapaxes(routes, 0, 1).reshape(-1)
    ranking = pair_ranks(ordered, experts).reshape(top_count, tok_rows)
    ordered = ordered.reshape(top_count, tok_rows)
    distance = lax.rem(ordered - me + devices, devices)
    slot_of = jnp.where(ranking < CAP, distance * CAP + ranking, -1)
    slot_ids = jnp.arange(slot_count, dtype=jnp.int32)
    pick = slot_of[:, None, :] == slot_ids[None, :, None]
    select = jnp.any(pick, axis=0).astype(jnp.bfloat16)
    pair_gates = jnp.swapaxes(route_gates, 0, 1).astype(jnp.float32)
    send_gate = jnp.einsum("kst,kt->s", pick.astype(jnp.float32), pair_gates)
    send_w = jnp.broadcast_to(send_gate[:, None], (slot_count, LANES)).astype(jnp.bfloat16)
    send_x = jnp.dot(select, saved_input, preferred_element_type=jnp.float32).astype(jnp.bfloat16)
    send_g = jnp.dot(select, grad_out, preferred_element_type=jnp.float32).astype(jnp.bfloat16)
    shape3 = (devices, CAP, features)
    back = exchange(
        send_x.reshape(shape3),
        send_g.reshape(shape3),
        send_w.reshape(devices, CAP, LANES),
        gate_proj[0],
        up_proj[0],
        down_proj[0],
    )
    total = jnp.einsum(
        "st,sd->td", select, back.reshape(slot_count, features), preferred_element_type=jnp.float32
    )
    return total.astype(jnp.bfloat16)


def solution(mesh):
    in_specs = (
        P(("dp", "expert"), None),
        P(("dp", "expert"), None),
        P(("dp", "expert"), None),
        P(("dp", "expert"), None),
        P("expert", None, None),
        P("expert", None, None),
        P("expert", None, None),
    )
    out_specs = P(("dp", "expert"), None)
    return jax.shard_map(body, mesh=mesh, in_specs=in_specs, out_specs=out_specs, check_vma=False)
```

profile of v0, /device:TPU:102, one launch (start us, length us, event | category | flops | bytes accessed | tf_op | source)
XLA Modules:
  0.0 248.7 jit_solution(6017709504374337551)
XLA Ops:
  0.0 0.0 copy-start
  0.0 0.8 fusion.7
  0.8 4.5 %reduce-window.6 = s32[16,8,128]{2,1,0:T(8,128)S(1)} reduce-window(s32[16,8,128]{2,1,0:T(8,128)S(1)} %fusion.7, s32[]{:T(128)} %constant.7.clone.1), window={size=1x1x128 pad=0_0x0_0x127_0}, to_apply=%region_0.0 | reduce-window | flops 2080768 | bytes 131076 | tf_op jit(solution)/shard_map/reduce-window
  5.3 0.1 slice.8
  5.3 0.1 copy.10
  5.5 0.1 copy.11
  5.6 0.1 broadcast_add_fusion
  5.7 0.7 fusion.6
  6.4 0.7 fusion.11
  7.1 1.4 fusion.3
  8.5 0.1 broadcast_in_dim.16
  8.6 0.0 copy-start.1
  8.6 0.6 fusion.1
  9.2 0.9 broadcast_in_dim.17.sw
  10.1 0.0 copy-done
  10.1 2.9 %convolution_convert_fusion = bf16[896,2048]{1,0:T(8,128)(2,1)} fusion(pred[896,128]{1,0:T(8,128)(4,1)S(1)} %fusion.1, bf16[128,2048]{1,0:T(8,128)(2,1)S(1)} %copy-done), kind=kOutput, calls=%fused_computation.3 | convolution fusion | flops 471597056 | bytes 4308992 | tf_op jit(solution)/shard_map/dot_general | solution.py:151
  13.0 0.0 copy-done.1
  13.0 2.9 %convolution_convert_fusion.1 = bf16[896,2048]{1,0:T(8,128)(2,1)} fusion(pred[896,128]{1,0:T(8,128)(4,1)S(1)} %fusion.1, bf16[128,2048]{1,0:T(8,128)(2,1)S(1)} %copy-done.1), kind=kOutput, calls=%fused_computation.4 | convolution fusion | flops 471597056 | bytes 4308992 | tf_op jit(solution)/shard_map/dot_general | solution.py:150
  15.9 229.2 %shard_map.73 = bf16[16,56,2048]{2,1,0:T(8,128)(2,1)} custom-call(bf16[16,56,2048]{2,1,0:T(8,128)(2,1)} %bitcast.43, bf16[16,56,2048]{2,1,0:T(8,128)(2,1)} %bitcast.42, bf16[16,56,128]{2,1,0:T(8,128)(2,1)} %broadcast_in_dim.17.sw, bf16[2048,768]{1,0:T(8,128)(2,1)} %bitcast.49, bf16[2048,768]{1,0:T(8,128)(2,1)} %bitcast.50, bf16[768,2048]{1,0:T(8,128)(2,1)} %bitcast.51), custom_call_target="tpu_custom_call" | custom-call | flops 14092861440 | bytes 14680064 | tf_op jit(solution)/shard_map/pallas_call | solution.py:105
  245.1 3.6 %convolution_convert_fusion.2 = bf16[128,2048]{1,0:T(8,128)(2,1)} fusion(pred[896,128]{1,0:T(8,128)(4,1)S(1)} %fusion.1, bf16[896,2048]{1,0:T(8,128)(2,1)} %bitcast.44), kind=kOutput, calls=%fused_computation.5 | convolution fusion | flops 470024192 | bytes 4308992 | tf_op jit(solution)/shard_map/st,sd->td/dot_general | solution.py:161
  (2 shorter events, 0.0 us)
Async XLA Ops:
  0.0 10.1 %copy-start = (bf16[128,2048]{1,0:T(8,128)(2,1)S(1)}, bf16[128,2048]{1,0:T(8,128)(2,1)}, u32[]{:S(2)}) copy-start(bf16[128,2048]{1,0:T(8,128)(2,1)} %param.8) | copy-start | bytes 1572868
  8.6 4.4 %copy-start.1 = (bf16[128,2048]{1,0:T(8,128)(2,1)S(1)}, bf16[128,2048]{1,0:T(8,128)(2,1)}, u32[]{:S(2)}) copy-start(bf16[128,2048]{1,0:T(8,128)(2,1)} %param.7) | copy-start | bytes 1572868
where the time goes:
time: 250 us; the launch traced here: 249 us
  Pallas kernels  229 us (92%)
  matrix products  10.8 us (4%)
  other arithmetic  7.37 us (3%)
    pallas_call x1, Pallas kernels, exchange(): pl.pallas_call(functools.partial(moe_kernel, n), out_shape=jax.ShapeDtype...  229 us

commit v1 on v0

--- a/solution.py
+++ b/solution.py
@@ -9,6 +9,7 @@
 
 CAP = 56
 LANES = 128
+PIECES = 8
 MESH_ID = pl.DeviceIdType.MESH
 
 
@@ -52,24 +53,36 @@
     srcs = (sx, sg, sw)
     dsts = (rx, rg, rw)
 
-    def dispatch(k, d):
+    def dispatch(k, d, cols=None):
+        src, dst = srcs[k].at[d], dsts[k].at[d]
+        if cols is not None:
+            src, dst = src.at[:, cols], dst.at[:, cols]
         return pltpu.make_async_remote_copy(
-            srcs[k].at[d], dsts[k].at[d], dsend.at[k, d], drecv.at[k, d],
+            src, dst, dsend.at[k, d], drecv.at[k, d],
             device_id=peer(d), device_id_type=MESH_ID,
         )
 
-    def give_back(d):
+    def give_back(d, cols=None):
+        src, dst = ob.at[d], ret.at[d]
+        if cols is not None:
+            src, dst = src.at[:, cols], dst.at[:, cols]
         return pltpu.make_async_remote_copy(
-            ob.at[d], ret.at[d], bsend.at[d], brecv.at[d],
+            src, dst, bsend.at[d], brecv.at[d],
             device_id=back_peer(d), device_id_type=MESH_ID,
         )
+
+    features = sx.shape[-1]
+    width = features // PIECES
+    pieces = [pl.ds(j * width, width) for j in range(PIECES)]
 
     local_in = [pltpu.make_async_copy(srcs[k].at[0], dsts[k].at[0], lsem.at[k]) for k in range(3)]
     for c in local_in:
         c.start()
     for d in range(1, n):
-        for k in range(3):
-            dispatch(k, d).start()
+        for cols in pieces:
+            dispatch(0, d, cols).start()
+            dispatch(1, d, cols).start()
+        dispatch(2, d).start()
 
     for c in local_in:
         c.wait()
@@ -81,7 +94,8 @@
         for k in range(3):
             dispatch(k, d).wait_recv()
         ob[d] = expert_block(rx[d], rg[d], rw[d], wg, wu, wd)
-        give_back(d).start()
+        for cols in pieces:
+            give_back(d, cols).start()
         return carry
 
     lax.fori_loop(1, n, step, 0)

time: 250 us -> 250 us (level)
  no operation moved by 1% of the time
where the time goes in v1:
time: 250 us; the launch traced here: 249 us
  Pallas kernels  229 us (92%)
  matrix products  10.8 us (4%)
  other arithmetic  7.37 us (3%)
    pallas_call x1, Pallas kernels, exchange(): pl.pallas_call(functools.partial(moe_kernel, n), out_shape=jax.ShapeDtype...  229 us

profile of v1, /device:TPU:102, one launch (start us, length us, event | category | flops | bytes accessed | tf_op | source)
XLA Modules:
  0.0 248.9 jit_solution(17904934710070068043)
XLA Ops:
  0.0 0.0 copy-start
  0.0 0.8 fusion.7
  0.8 4.5 %reduce-window.6 = s32[16,8,128]{2,1,0:T(8,128)S(1)} reduce-window(s32[16,8,128]{2,1,0:T(8,128)S(1)} %fusion.7, s32[]{:T(128)} %constant.7.clone.1), window={size=1x1x128 pad=0_0x0_0x127_0}, to_apply=%region_0.0 | reduce-window | flops 2080768 | bytes 131076 | tf_op jit(solution)/shard_map/reduce-window
  5.3 0.1 slice.8
  5.3 0.1 copy.10
  5.5 0.1 copy.11
  5.6 0.1 broadcast_add_fusion
  5.7 0.7 fusion.6
  6.4 0.7 fusion.11
  7.1 1.4 fusion.3
  8.5 0.1 broadcast_in_dim.16
  8.6 0.0 copy-start.1
  8.6 0.6 fusion.1
  9.2 0.9 broadcast_in_dim.17.sw
  10.1 0.0 copy-done
  10.1 2.9 %convolution_convert_fusion = bf16[896,2048]{1,0:T(8,128)(2,1)} fusion(pred[896,128]{1,0:T(8,128)(4,1)S(1)} %fusion.1, bf16[128,2048]{1,0:T(8,128)(2,1)S(1)} %copy-done), kind=kOutput, calls=%fused_computation.3 | convolution fusion | flops 471597056 | bytes 4308992 | tf_op jit(solution)/shard_map/dot_general | solution.py:165
  13.0 0.0 copy-done.1
  13.0 2.9 %convolution_convert_fusion.1 = bf16[896,2048]{1,0:T(8,128)(2,1)} fusion(pred[896,128]{1,0:T(8,128)(4,1)S(1)} %fusion.1, bf16[128,2048]{1,0:T(8,128)(2,1)S(1)} %copy-done.1), kind=kOutput, calls=%fused_computation.4 | convolution fusion | flops 471597056 | bytes 4308992 | tf_op jit(solution)/shard_map/dot_general | solution.py:164
  15.9 229.4 %shard_map.73 = bf16[16,56,2048]{2,1,0:T(8,128)(2,1)} custom-call(bf16[16,56,2048]{2,1,0:T(8,128)(2,1)} %bitcast.43, bf16[16,56,2048]{2,1,0:T(8,128)(2,1)} %bitcast.42, bf16[16,56,128]{2,1,0:T(8,128)(2,1)} %broadcast_in_dim.17.sw, bf16[2048,768]{1,0:T(8,128)(2,1)} %bitcast.49, bf16[2048,768]{1,0:T(8,128)(2,1)} %bitcast.50, bf16[768,2048]{1,0:T(8,128)(2,1)} %bitcast.51), custom_call_target="tpu_custom_call" | custom-call | flops 14092861440 | bytes 14680064 | tf_op jit(solution)/shard_map/pallas_call | solution.py:119
  245.3 3.6 %convolution_convert_fusion.2 = bf16[128,2048]{1,0:T(8,128)(2,1)} fusion(pred[896,128]{1,0:T(8,128)(4,1)S(1)} %fusion.1, bf16[896,2048]{1,0:T(8,128)(2,1)} %bitcast.44), kind=kOutput, calls=%fused_computation.5 | convolution fusion | flops 470024192 | bytes 4308992 | tf_op jit(solution)/shard_map/st,sd->td/dot_general | solution.py:175
  (2 shorter events, 0.0 us)
Async XLA Ops:
  0.0 10.1 %copy-start = (bf16[128,2048]{1,0:T(8,128)(2,1)S(1)}, bf16[128,2048]{1,0:T(8,128)(2,1)}, u32[]{:S(2)}) copy-start(bf16[128,2048]{1,0:T(8,128)(2,1)} %param.8) | copy-start | bytes 1572868
  8.6 4.4 %copy-start.1 = (bf16[128,2048]{1,0:T(8,128)(2,1)S(1)}, bf16[128,2048]{1,0:T(8,128)(2,1)}, u32[]{:S(2)}) copy-start(bf16[128,2048]{1,0:T(8,128)(2,1)} %param.7) | copy-start | bytes 1572868

commit v2 on v1

--- a/solution.py
+++ b/solution.py
@@ -9,7 +9,7 @@
 
 CAP = 56
 LANES = 128
-PIECES = 8
+PIECES = 7
 MESH_ID = pl.DeviceIdType.MESH
 
 
@@ -56,7 +56,7 @@
     def dispatch(k, d, cols=None):
         src, dst = srcs[k].at[d], dsts[k].at[d]
         if cols is not None:
-            src, dst = src.at[:, cols], dst.at[:, cols]
+            src, dst = src.at[cols], dst.at[cols]
         return pltpu.make_async_remote_copy(
             src, dst, dsend.at[k, d], drecv.at[k, d],
             device_id=peer(d), device_id_type=MESH_ID,
@@ -65,15 +65,14 @@
     def give_back(d, cols=None):
         src, dst = ob.at[d], ret.at[d]
         if cols is not None:
-            src, dst = src.at[:, cols], dst.at[:, cols]
+            src, dst = src.at[cols], dst.at[cols]
         return pltpu.make_async_remote_copy(
             src, dst, bsend.at[d], brecv.at[d],
             device_id=back_peer(d), device_id_type=MESH_ID,
         )
 
-    features = sx.shape[-1]
-    width = features // PIECES
-    pieces = [pl.ds(j * width, width) for j in range(PIECES)]
+    height = sx.shape[1] // PIECES
+    pieces = [pl.ds(j * height, height) for j in range(PIECES)]
 
     local_in = [pltpu.make_async_copy(srcs[k].at[0], dsts[k].at[0], lsem.at[k]) for k in range(3)]
     for c in local_in:

time: 250 us -> 250 us (level)
  no operation moved by 1% of the time
where the time goes in v2:
time: 250 us; the launch traced here: 249 us
  Pallas kernels  229 us (92%)
  matrix products  10.8 us (4%)
  other arithmetic  7.37 us (3%)
    pallas_call x1, Pallas kernels, exchange(): pl.pallas_call(functools.partial(moe_kernel, n), out_shape=jax.ShapeDtype...  229 us

profile of v2, /device:TPU:102, one launch (start us, length us, event | category | flops | bytes accessed | tf_op | source)
XLA Modules:
  0.0 249.0 jit_solution(9373887552764495696)
XLA Ops:
  0.0 0.0 copy-start
  0.0 0.8 fusion.7
  0.8 4.5 %reduce-window.6 = s32[16,8,128]{2,1,0:T(8,128)S(1)} reduce-window(s32[16,8,128]{2,1,0:T(8,128)S(1)} %fusion.7, s32[]{:T(128)} %constant.7.clone.1), window={size=1x1x128 pad=0_0x0_0x127_0}, to_apply=%region_0.0 | reduce-window | flops 2080768 | bytes 131076 | tf_op jit(solution)/shard_map/reduce-window
  5.3 0.1 slice.8
  5.3 0.1 copy.10
  5.5 0.1 copy.11
  5.6 0.1 broadcast_add_fusion
  5.7 0.7 fusion.6
  6.4 0.7 fusion.11
  7.1 1.4 fusion.3
  8.5 0.1 broadcast_in_dim.16
  8.6 0.0 copy-start.1
  8.6 0.6 fusion.1
  9.2 0.9 broadcast_in_dim.17.sw
  10.1 0.0 copy-done
  10.1 2.9 %convolution_convert_fusion = bf16[896,2048]{1,0:T(8,128)(2,1)} fusion(pred[896,128]{1,0:T(8,128)(4,1)S(1)} %fusion.1, bf16[128,2048]{1,0:T(8,128)(2,1)S(1)} %copy-done), kind=kOutput, calls=%fused_computation.3 | convolution fusion | flops 471597056 | bytes 4308992 | tf_op jit(solution)/shard_map/dot_general | solution.py:164
  13.0 0.0 copy-done.1
  13.0 2.9 %convolution_convert_fusion.1 = bf16[896,2048]{1,0:T(8,128)(2,1)} fusion(pred[896,128]{1,0:T(8,128)(4,1)S(1)} %fusion.1, bf16[128,2048]{1,0:T(8,128)(2,1)S(1)} %copy-done.1), kind=kOutput, calls=%fused_computation.4 | convolution fusion | flops 471597056 | bytes 4308992 | tf_op jit(solution)/shard_map/dot_general | solution.py:163
  15.9 229.5 %shard_map.73 = bf16[16,56,2048]{2,1,0:T(8,128)(2,1)} custom-call(bf16[16,56,2048]{2,1,0:T(8,128)(2,1)} %bitcast.43, bf16[16,56,2048]{2,1,0:T(8,128)(2,1)} %bitcast.42, bf16[16,56,128]{2,1,0:T(8,128)(2,1)} %broadcast_in_dim.17.sw, bf16[2048,768]{1,0:T(8,128)(2,1)} %bitcast.49, bf16[2048,768]{1,0:T(8,128)(2,1)} %bitcast.50, bf16[768,2048]{1,0:T(8,128)(2,1)} %bitcast.51), custom_call_target="tpu_custom_call" | custom-call | flops 14092861440 | bytes 14680064 | tf_op jit(solution)/shard_map/pallas_call | solution.py:118
  245.4 3.6 %convolution_convert_fusion.2 = bf16[128,2048]{1,0:T(8,128)(2,1)} fusion(pred[896,128]{1,0:T(8,128)(4,1)S(1)} %fusion.1, bf16[896,2048]{1,0:T(8,128)(2,1)} %bitcast.44), kind=kOutput, calls=%fused_computation.5 | convolution fusion | flops 470024192 | bytes 4308992 | tf_op jit(solution)/shard_map/st,sd->td/dot_general | solution.py:174
  (2 shorter events, 0.0 us)
Async XLA Ops:
  0.0 10.1 %copy-start = (bf16[128,2048]{1,0:T(8,128)(2,1)S(1)}, bf16[128,2048]{1,0:T(8,128)(2,1)}, u32[]{:S(2)}) copy-start(bf16[128,2048]{1,0:T(8,128)(2,1)} %param.8) | copy-start | bytes 1572868
  8.6 4.4 %copy-start.1 = (bf16[128,2048]{1,0:T(8,128)(2,1)S(1)}, bf16[128,2048]{1,0:T(8,128)(2,1)}, u32[]{:S(2)}) copy-start(bf16[128,2048]{1,0:T(8,128)(2,1)} %param.7) | copy-start | bytes 1572868

commit v3 on v2

--- a/solution.py
+++ b/solution.py
@@ -78,10 +78,11 @@
     for c in local_in:
         c.start()
     for d in range(1, n):
-        for cols in pieces:
-            dispatch(0, d, cols).start()
-            dispatch(1, d, cols).start()
         dispatch(2, d).start()
+    for cols in pieces:
+        for k in range(2):
+            for d in range(1, n):
+                dispatch(k, d, cols).start()
 
     for c in local_in:
         c.wait()

time: 250 us -> 183 us (0.73); the launches traced: 249 us -> 179 us
  Pallas kernels: 229 us -> 160 us
    pallas_call x1, Pallas kernels: 229 us -> 160 us  [exchange(): pl.pallas_call(functools.partial(moe_kernel, n), out_shape=jax.ShapeDtype...]
where the time goes in v3:
time: 183 us; the launch traced here: 179 us
  Pallas kernels  160 us (87%)
  matrix products  10.8 us (6%)
  other arithmetic  7.37 us (4%)
    pallas_call x1, Pallas kernels, exchange(): pl.pallas_call(functools.partial(moe_kernel, n), out_shape=jax.ShapeDtype...  160 us
    another operation x3, other arithmetic  4.61 us

profile of v3, /device:TPU:102, one launch (start us, length us, event | category | flops | bytes accessed | tf_op | source)
XLA Modules:
  0.0 179.3 jit_solution(9152560183825610222)
XLA Ops:
  0.0 0.0 copy-start
  0.0 0.8 fusion.7
  0.8 4.5 %reduce-window.6 = s32[16,8,128]{2,1,0:T(8,128)S(1)} reduce-window(s32[16,8,128]{2,1,0:T(8,128)S(1)} %fusion.7, s32[]{:T(128)} %constant.7.clone.1), window={size=1x1x128 pad=0_0x0_0x127_0}, to_apply=%region_0.0 | reduce-window | flops 2080768 | bytes 131076 | tf_op jit(solution)/shard_map/reduce-window
  5.3 0.1 slice.8
  5.3 0.1 copy.10
  5.5 0.1 copy.11
  5.6 0.1 broadcast_add_fusion
  5.7 0.7 fusion.6
  6.4 0.7 fusion.11
  7.1 1.4 fusion.3
  8.5 0.1 broadcast_in_dim.16
  8.6 0.0 copy-start.1
  8.6 0.6 fusion.1
  9.2 0.9 broadcast_in_dim.17.sw
  10.1 0.0 copy-done
  10.1 2.9 %convolution_convert_fusion = bf16[896,2048]{1,0:T(8,128)(2,1)} fusion(pred[896,128]{1,0:T(8,128)(4,1)S(1)} %fusion.1, bf16[128,2048]{1,0:T(8,128)(2,1)S(1)} %copy-done), kind=kOutput, calls=%fused_computation.3 | convolution fusion | flops 471597056 | bytes 4308992 | tf_op jit(solution)/shard_map/dot_general | solution.py:165
  13.0 0.0 copy-done.1
  13.0 2.9 %convolution_convert_fusion.1 = bf16[896,2048]{1,0:T(8,128)(2,1)} fusion(pred[896,128]{1,0:T(8,128)(4,1)S(1)} %fusion.1, bf16[128,2048]{1,0:T(8,128)(2,1)S(1)} %copy-done.1), kind=kOutput, calls=%fused_computation.4 | convolution fusion | flops 471597056 | bytes 4308992 | tf_op jit(solution)/shard_map/dot_general | solution.py:164
  15.9 159.8 %shard_map.73 = bf16[16,56,2048]{2,1,0:T(8,128)(2,1)} custom-call(bf16[16,56,2048]{2,1,0:T(8,128)(2,1)} %bitcast.43, bf16[16,56,2048]{2,1,0:T(8,128)(2,1)} %bitcast.42, bf16[16,56,128]{2,1,0:T(8,128)(2,1)} %broadcast_in_dim.17.sw, bf16[2048,768]{1,0:T(8,128)(2,1)} %bitcast.49, bf16[2048,768]{1,0:T(8,128)(2,1)} %bitcast.50, bf16[768,2048]{1,0:T(8,128)(2,1)} %bitcast.51), custom_call_target="tpu_custom_call" | custom-call | flops 14092861440 | bytes 14680064 | tf_op jit(solution)/shard_map/pallas_call | solution.py:119
  175.7 3.6 %convolution_convert_fusion.2 = bf16[128,2048]{1,0:T(8,128)(2,1)} fusion(pred[896,128]{1,0:T(8,128)(4,1)S(1)} %fusion.1, bf16[896,2048]{1,0:T(8,128)(2,1)} %bitcast.44), kind=kOutput, calls=%fused_computation.5 | convolution fusion | flops 470024192 | bytes 4308992 | tf_op jit(solution)/shard_map/st,sd->td/dot_general | solution.py:175
  (2 shorter events, 0.0 us)
Async XLA Ops:
  0.0 10.1 %copy-start = (bf16[128,2048]{1,0:T(8,128)(2,1)S(1)}, bf16[128,2048]{1,0:T(8,128)(2,1)}, u32[]{:S(2)}) copy-start(bf16[128,2048]{1,0:T(8,128)(2,1)} %param.8) | copy-start | bytes 1572868
  8.6 4.4 %copy-start.1 = (bf16[128,2048]{1,0:T(8,128)(2,1)S(1)}, bf16[128,2048]{1,0:T(8,128)(2,1)}, u32[]{:S(2)}) copy-start(bf16[128,2048]{1,0:T(8,128)(2,1)} %param.7) | copy-start | bytes 1572868
